TPU v7x, 32 devices: a whole 2x2x4 slice. The times are simulated.
32 devices in a mesh: cell: 16 (over z, y, x), win: 2 (over core).
Axes of the slice: x: 2, y: 2, z: 4, core: 2. Of those that a mesh axis runs over, the one named last changes fastest.
Arguments:
- anomalies: bfloat16 [256, 60, 8192], P('win', None, 'cell'), may hold values from -6 to 6
- eofs: bfloat16 [100, 60, 8192], P('win', None, 'cell'), may hold values from -0.015625 to 0.015625
- cell_area: float32 [8192], P('cell'), may hold values from 0.5 to 2
- levels: int32 [8192], P('cell'), may hold values from 1 to 60
- counts: int32 [16], replicated, may hold values from 128 to 512, as said below
Outputs:
- pcs: float32 [256, 100], P('win')
- regression: float32 [100, 8192], P('win', 'cell')
Inputs may be any that keep to these rules, and one draw needn't show every extreme that they name: `counts`: every entry is at most 512, and some block holds exactly 512 real cells.
All inputs are finite; a program needn't handle non-finite values.
Results may differ from a plain program's by a relative error of at most 0.0049.
Values may be sent and summed in bfloat16 or wider, within the bound.
No kernel may reach another device: no remote copies, remote signals or barrier semaphores. Data moves between devices by JAX's collectives and lax.ppermute only.
A program may use at most 64 MiB of HBM per device.

v0:
```python
import jax
import jax.numpy as jnp
from jax import lax
from jax.sharding import PartitionSpec as P


def shards(anomalies, eofs, cell_area, levels, counts):
    steps_here, depth_count, slots = anomalies.shape
    position = lax.axis_index("cell")
    filled = counts[position]
    live = jnp.arange(slots, dtype=jnp.int32) < filled
    depth = jnp.arange(depth_count, dtype=jnp.int32)[:, None] < levels[None, :]
    mask = (live[None, :] & depth).astype(jnp.float32)
    weighted = (eofs.astype(jnp.float32) * (cell_area[None, :] * mask)[None]).astype(jnp.bfloat16)
    flat_data = anomalies.reshape(steps_here, depth_count * slots)
    piece = lax.all_gather(weighted, "win", axis=0, tiled=True)
    flat_piece = piece.reshape(piece.shape[0], depth_count * slots)
    partial_value = lax.dot_general(
        flat_data, flat_piece, (((1,), (1,)), ((), ())), preferred_element_type=jnp.float32
    )
    pcs = lax.psum(partial_value, "cell")
    column = jnp.sum(anomalies.astype(jnp.float32) * mask[None], axis=1).astype(jnp.bfloat16)
    pcs_rounded = pcs.astype(jnp.bfloat16)
    windows = lax.axis_size("win")
    term = lax.dot_general(
        pcs_rounded, column, (((0,), (0,)), ((), ())), preferred_element_type=jnp.float32
    )
    term = term / jnp.sqrt(jnp.float32(steps_here * windows))
    regression = lax.psum_scatter(term, "win", scatter_dimension=0, tiled=True)
    return (pcs, regression)


def solution(mesh):
    in_specs = (P("win", None, "cell"), P("win", None, "cell"), P("cell"), P("cell"), P())
    out_specs = (P("win", None), P("win", "cell"))
    return jax.shard_map(shards, mesh=mesh, in_specs=in_specs, out_specs=out_specs, check_vma=False)
```

profile of v0, /device:TPU:0, one launch (start us, length us, event | category | flops | bytes accessed | tf_op | source)
XLA Modules:
  0.0 138.4 jit_solution(9140950876646721835)
XLA Ops:
  7.2 0.0 copy-start.1
  7.2 0.0 all-gather.2.cloned.1.call-start
  7.2 1.2 dynamic_slice.3
  8.5 0.6 iota_compare_fusion.1
  9.1 0.7 fusion.9
  9.9 4.6 %multiply_convert_fusion = bf16[50,60,512]{2,1,0:T(8,128)(2,1)} fusion(bf16[50,60,512]{2,1,0:T(8,128)(2,1)} %param.6, f32[60,512]{1,0:T(8,128)S(1)} %fusion.9), kind=kLoop, calls=%fused_computation.1 | loop fusion | flops 4608000 | bytes 6266880 | tf_op jit(solution)/shard_map/convert_element_type | solution.py:14
  14.5 0.0 all-gather.2.cloned.1.call-update
  14.5 0.0 copy-done.1
  14.5 5.0 %multiply_reduce_fusion = bf16[128,512]{1,0:T(8,128)(2,1)S(1)} fusion(bf16[128,60,512]{2,0,1:T(8,128)(2,1)} %param.5, f32[60,512]{1,0:T(8,128)S(1)} %fusion.8), kind=kLoop, calls=%fused_computation | loop fusion | flops 11730944 | bytes 8118272 | tf_op jit(solution)/shard_map/reduce_sum | solution.py:22
  19.5 0.0 copy-start.2
  19.5 15.0 %all-gather.2.cloned.1.call-done = bf16[100,60,512]{2,1,0:T(8,128)(2,1)} async-done(((bf16[50,60,512]{2,1,0:T(8,128)(2,1)}), bf16[100,60,512]{2,1,0:T(8,128)(2,1)}) %all-gather.2.cloned.1.call-update) | async-done | bytes 6144016 | tf_op jit(solution)/shard_map/all_gather | solution.py:16
  34.5 12.3 %fusion.3 = f32[128,100]{0,1:T(8,128)S(1)} fusion(bf16[128,60,512]{2,0,1:T(8,128)(2,1)} %param.5, bf16[100,60,512]{2,1,0:T(8,128)(2,1)} %all-gather.2.cloned.1.call-done), kind=kOutput, calls=%fused_computation.5 | convolution fusion | flops 786432000 | bytes 14059520 | tf_op jit(solution)/shard_map/dot_general | solution.py:18
  46.8 77.1 %psum.7 = f32[128,100]{0,1:T(8,128)S(1)} all-reduce(f32[128,100]{0,1:T(8,128)S(1)} %fusion.3), channel_id=1, replica_groups=mesh['cell'=16,'win'=2] {'cell'}, use_global_device_ids=true, to_apply=%region_0.0 | all-reduce | flops 12800 | bytes 102400 | tf_op jit(solution)/shard_map/psum | solution.py:21
  123.9 0.0 copy-start
  123.9 0.2 convolution_multiply_fusion
  124.1 3.1 %fusion = f32[56,512]{1,0:T(8,128)S(1)} fusion(f32[100,512]{1,0:T(8,128)S(1)} %convolution_multiply_fusion), kind=kCustom, calls=%all-reduce-scatter | all-reduce-scatter fusion | flops 57345 | bytes 320000
  127.1 2.3 %collective-permute-start = (f32[6,512]{1,0:T(8,128)S(1)}, f32[6,512]{1,0:T(8,128)S(1)}, u32[]{:S(2)}, u32[]{:S(2)}) collective-permute-start(f32[6,512]{1,0:T(8,128)S(1)} %slice), channel_id=1, source_target_pairs={{0,1},{2,3},{4,5},{6,7},{8,9},{10,11},{12,13},{14,15},{16,17},{18,... | collective-permute-start | bytes 36872
  129.4 0.0 copy-done.2
  129.4 0.6 dynamic-slice.4
  130.7 0.0 collective-permute-done
  130.7 0.2 concatenate
  130.9 0.7 constant_dynamic-slice_fusion
  131.5 0.0 copy-done
  (2 shorter events, 0.0 us)
Async XLA Ops:
  7.2 7.3 %copy-start.1 = (s32[512]{0:T(512)S(1)}, s32[512]{0:T(512)}, u32[]{:S(2)}) copy-start(s32[512]{0:T(512)} %param.8) | copy-start | bytes 6148
  7.2 27.3 %all-gather.2.cloned.1.call-start = ((), (), s32[]{:S(2)}) async-start(), calls=%async_computation | async-start | bytes 9830400 | tf_op jit(solution)/shard_map/all_gather | solution.py:16
  19.5 109.9 %copy-start.2 = (u32[32]{0:T(128)S(1)}, u32[32]{0:T(128)}, u32[]{:S(2)}) copy-start(u32[32]{0:T(128)} %constant.18) | copy-start | bytes 388
  123.9 7.6 %copy-start = (f32[128,100]{0,1:T(8,128)}, f32[128,100]{0,1:T(8,128)S(1)}, u32[]{:S(2)}) copy-start(f32[128,100]{0,1:T(8,128)S(1)} %psum.7) | copy-start | bytes 153604
  127.1 3.5 %collective-permute-start = (f32[6,512]{1,0:T(8,128)S(1)}, f32[6,512]{1,0:T(8,128)S(1)}, u32[]{:S(2)}, u32[]{:S(2)}) collective-permute-start(f32[6,512]{1,0:T(8,128)S(1)} %slice), channel_id=1, source_target_pairs={{0,1},{2,3},{4,5},{6,7},{8,9},{10,11},{12,13},{14,15},{16,17},{18,... | collective-permute-start | bytes 36872
Sparse Core Ops, SparseCore 0:
  14.6 19.8 all-gather.1
where the time goes:
time: 139 us; the launch traced here: 138 us
  blocking collectives  80.2 us (58%)
  waiting for transfers between devices  15 us (11%)
  between operations  14.8 us (11%)
  matrix products  12.4 us (9%)
  other arithmetic  11 us (8%)
  local copies, waits for them, and re-layouts  2.69 us (2%)
  starting transfers between devices  2.3 us (2%)
    psum x1, blocking collectives, shards(): pcs = lax.psum(partial_value, 'cell')  77.1 us
    all_gather x1, waiting for transfers between devices, shards(): piece = lax.all_gather(weighted, 'win', axis=0, tiled=True)  15 us
    dot_general x1, matrix products, shards(): lax.dot_general(flat_data, flat_piece, (((1,), (1,)), ((), ())), preferre...  12.3 us
    reduce_sum x1, other arithmetic, shards(): jnp.sum(anomalies.astype(jnp.float32) * mask[None], axis=1)  5.01 us
    convert_element_type x1, other arithmetic, shards(): (eofs.astype(jnp.float32) * (cell_area[None, :] * mask)[None]).astype(jnp...  4.6 us
    unnamed x1, blocking collectives  3.06 us
  transfers between devices with their start and end apart: 2, of which 1 were waited for; matrix products, arithmetic and copies ran while one was open for 4% of the time, Pallas kernels for 0%

commit v1 on v0

v1 whole, which is shorter than its diff:
```python
import jax
import jax.numpy as jnp
from jax import lax
from jax.sharding import PartitionSpec as P


def exchange_sum(value, size):
    step = 1
    while step < size:
        if size % (4 * step) == 0:
            far, side, near = [
                lax.ppermute(value, "cell", [(i, i ^ k) for i in range(size)]) for k in (3 * step, 2 * step, step)
            ]
            value = (value + near) + (side + far)
            step *= 4
        else:
            value = value + lax.ppermute(value, "cell", [(i, i ^ step) for i in range(size)])
            step *= 2
    return value


def sum_cells(value, size):
    if size & (size - 1):
        return lax.psum(value, "cell")
    return exchange_sum(value, size)


def swap(value):
    return lax.ppermute(value, "win", [(0, 1), (1, 0)])


def make(cells):
    def shards(anomalies, eofs, cell_area, levels, counts):
        steps_here, depth_count, slots = anomalies.shape
        own = eofs.shape[0]
        filled = counts[lax.axis_index("cell")]
        window = lax.axis_index("win")
        other_eofs = swap(eofs)
        live = jnp.arange(slots, dtype=jnp.int32) < filled
        depth = jnp.arange(depth_count, dtype=jnp.int32)[:, None] < levels[None, :]
        mask = (live[None, :] & depth).astype(jnp.float32)
        scale = (cell_area[None, :] * mask)[None]
        column = jnp.sum(anomalies.astype(jnp.float32) * mask[None], axis=1).astype(jnp.bfloat16)
        other_column = swap(column)
        flat = anomalies.reshape(steps_here, depth_count * slots)

        def project(patterns):
            weighted = (patterns.astype(jnp.float32) * scale).astype(jnp.bfloat16)
            return lax.dot_general(
                flat, weighted.reshape(own, depth_count * slots), (((1,), (1,)), ((), ())), preferred_element_type=jnp.float32
            )

        total = sum_cells(jnp.concatenate([project(eofs), project(other_eofs)], axis=1), cells)
        mine, others = total[:, :own], total[:, own:]
        pcs = jnp.where(window == 0, total, jnp.concatenate([others, mine], axis=1))
        arrived = swap(others.astype(jnp.bfloat16))
        terms = lax.dot_general(
            mine.astype(jnp.bfloat16), column, (((0,), (0,)), ((), ())), preferred_element_type=jnp.float32
        ) + lax.dot_general(arrived, other_column, (((0,), (0,)), ((), ())), preferred_element_type=jnp.float32)
        return pcs, terms / jnp.sqrt(jnp.float32(steps_here * 2))

    return shards


def solution(mesh):
    in_specs = (P("win", None, "cell"), P("win", None, "cell"), P("cell"), P("cell"), P())
    out_specs = (P("win", None), P("win", "cell"))
    return jax.shard_map(
        make(mesh.shape["cell"]), mesh=mesh, in_specs=in_specs, out_specs=out_specs, check_vma=False
    )
```

time: 139 us -> 40.6 us (0.29)
  blocking collectives: 80.2 us -> 0 us
  between operations: 14.8 us -> 0.76 us
  starting transfers between devices: 2.3 us -> 9.6 us
  matrix products: 12.4 us -> 8.92 us
  waiting for transfers between devices: 15 us -> 11.9 us
  other arithmetic: 11 us -> 7.98 us
  local copies, waits for them, and re-layouts: 2.69 us -> 1.27 us
    psum x1 -> x0, blocking collectives: 77.1 us -> none  [shards(): pcs = lax.psum(partial_value, 'cell')]
    all_gather x1 -> x0, waiting for transfers between devices: 15 us -> none  [shards(): piece = lax.all_gather(weighted, 'win', axis=0, tiled=True)]
    ppermute x0 -> x9, waiting for transfers between devices: none -> 11.9 us  [the longest x6 8.31 us: exchange_sum(): lax.ppermute(value, 'cell', [(i, i ^ k) for i in range(size)])]
    ppermute x0 -> x9, starting transfers between devices: none -> 9.6 us  [the longest x6 8.9 us: exchange_sum(): lax.ppermute(value, 'cell', [(i, i ^ k) for i in range(size)])]
    dot_general x2 -> x4, matrix products: 12.4 us -> 8.92 us  [the longest x2 7.98 us: project(): lax.dot_general(flat, weighted.reshape(own, depth_count * slots), (((1,),...]
    unnamed x1 -> x0, blocking collectives: 3.06 us -> none
    reduce_sum x1, other arithmetic: 5.01 us -> 2.29 us  [shards(): jnp.sum(anomalies.astype(jnp.float32) * mask[None], axis=1)]
    unnamed x1 -> x0, starting transfers between devices: 2.26 us -> none
  transfers between devices with their start and end apart: 2 -> 9, of which waited for: 1 -> 7; matrix products, arithmetic and copies ran while one was open for 4% -> 14% of each run, Pallas kernels for 0% -> 0%
where the time goes in v1:
time: 40.6 us; the launch traced here: 40.4 us
  waiting for transfers between devices  11.9 us (29%)
  starting transfers between devices  9.6 us (24%)
  matrix products  8.92 us (22%)
  other arithmetic  7.98 us (20%)
  local copies, waits for them, and re-layouts  1.27 us (3%)
  between operations  0.76 us (2%)
    ppermute x6, starting transfers between devices, exchange_sum(): lax.ppermute(value, 'cell', [(i, i ^ k) for i in range(size)])  8.9 us
    ppermute x6, waiting for transfers between devices, exchange_sum(): lax.ppermute(value, 'cell', [(i, i ^ k) for i in range(size)])  8.31 us
    dot_general x2, matrix products, project(): lax.dot_general(flat, weighted.reshape(own, depth_count * slots), (((1,),...  7.98 us
    convert_element_type x1, other arithmetic, project(): weighted = (patterns.astype(jnp.float32) * scale).astype(jnp.bfloat16)  3.6 us
    ppermute x3, waiting for transfers between devices, swap(): return lax.ppermute(value, 'win', [(0, 1), (1, 0)])  3.57 us
    reduce_sum x1, other arithmetic, shards(): jnp.sum(anomalies.astype(jnp.float32) * mask[None], axis=1)  2.29 us
    dynamic_slice x1, local copies, waits for them, and re-layouts, shards(): filled = counts[lax.axis_index('cell')]  1.24 us
    dot_general x1, matrix products, shards(): lax.dot_general(mine.astype(jnp.bfloat16), column, (((0,), (0,)), ((), ()...  0.81 us
  transfers between devices with their start and end apart: 9, of which 7 were waited for; matrix products, arithmetic and copies ran while one was open for 14% of the time, Pallas kernels for 0%

profile of v1, /device:TPU:0, one launch (start us, length us, event | category | flops | bytes accessed | tf_op | source)
XLA Modules:
  0.0 40.4 jit_solution(976778393267981284)
XLA Ops:
  0.6 0.6 %collective-permute-start = (bf16[50,60,512]{2,1,0:T(8,128)(2,1)}, bf16[50,60,512]{2,1,0:T(8,128)(2,1)S(1)}, u32[]{:S(2)}, u32[]{:S(2)}) collective-permute-start(bf16[50,60,512]{2,1,0:T(8,128)(2,1)} %param.6), channel_id=1, source_target_pairs={{0,1},{1,0},{2,3},{3,2},{4,5},{5,4},{6,7},{7,6},{8,9},{9,8},{10,11... | collective-permute-start | bytes 9216008 | tf_op jit(solution)/shard_map/ppermute | solution.py:29
  1.2 1.2 %dynamic_slice.3 = s32[1]{0:T(128)} dynamic-slice(s32[16]{0:T(128)} %param.9, s32[]{:T(128)S(6)} %select_n.12), dynamic_slice_sizes={1} | dynamic-slice | bytes 12 | tf_op jit(solution)/shard_map/dynamic_slice | solution.py:36
  2.4 0.6 %iota_compare_fusion.1 = pred[512]{0:T(512)(128)(4,1)S(1)} fusion(s32[]{:T(128)} %bitcast), kind=kLoop, calls=%fused_computation.20 | loop fusion | flops 512 | bytes 516 | tf_op jit(solution)/shard_map/lt | solution.py:39
  3.1 0.7 %fusion.13 = f32[60,512]{1,0:T(8,128)S(1)} fusion(f32[512]{0:T(512)} %param.7, s32[512]{0:T(512)} %param.8, pred[512]{0:T(512)(128)(4,1)S(1)} %iota_compare_fusion.1), kind=kLoop, calls=%fused_computation.14 | loop fusion | flops 92160 | bytes 127488 | tf_op jit(solution)/shard_map/mul | solution.py:42
  3.8 3.0 %collective-permute-done = bf16[50,60,512]{2,1,0:T(8,128)(2,1)S(1)} collective-permute-done((bf16[50,60,512]{2,1,0:T(8,128)(2,1)}, bf16[50,60,512]{2,1,0:T(8,128)(2,1)S(1)}, u32[]{:S(2)}, u32[]{:S(2)}) %collective-permute-start) | collective-permute-done | bytes 3072032 | tf_op jit(solution)/shard_map/ppermute | solution.py:29
  6.9 3.6 %multiply_convert_fusion.1 = (bf16[50,60,512]{2,1,0:T(8,128)(2,1)S(1)}, bf16[50,60,512]{2,1,0:T(8,128)(2,1)S(1)}) fusion(bf16[50,60,512]{2,1,0:T(8,128)(2,1)} %param.6, f32[60,512]{1,0:T(8,128)S(1)} %fusion.13, bf16[50,60,512]{2,1,0:T(8,128)(2,1)S(1)} %collective-permute-done), kind=kLoop, calls=%fused_computation.2 | loop fusion | flops 9216000 | bytes 12410880 | tf_op jit(solution)/shard_map/convert_element_type | solution.py:48
  10.5 4.0 %fusion.5 = f32[128,50]{0,1:T(8,128)S(1)} fusion(bf16[128,60,512]{2,0,1:T(8,128)(2,1)S(1)} %copy-done, bf16[50,60,512]{2,1,0:T(8,128)(2,1)S(1)} %get-tuple-element.2), kind=kOutput, calls=%fused_computation.9 | convolution fusion | flops 393216000 | bytes 10961920 | tf_op jit(solution)/shard_map/dot_general | solution.py:49
  14.5 4.0 %fusion.8 = f32[128,50]{0,1:T(8,128)S(1)} fusion(bf16[128,60,512]{2,0,1:T(8,128)(2,1)S(1)} %copy-done, bf16[50,60,512]{2,1,0:T(8,128)(2,1)S(1)} %get-tuple-element.3), kind=kOutput, calls=%fused_computation.10 | convolution fusion | flops 393216000 | bytes 10961920 | tf_op jit(solution)/shard_map/dot_general | solution.py:49
  18.5 2.9 %collective-permute-start.1 = (f32[128,100]{0,1:T(8,128)S(1)}, f32[128,100]{0,1:T(8,128)S(1)}, u32[]{:S(2)}, u32[]{:S(2)}) collective-permute-start(f32[128,100]{0,1:T(8,128)S(1)} %pad_maximum_fusion), channel_id=1, source_target_pairs={{0,2},{2,0},{4,6},{6,4},{8,10},{10,8},{12,14},{14,12},{16,18},{18,... | collective-permute-start | bytes 153608 | tf_op jit(solution)/shard_map/ppermute | solution.py:12
  21.4 1.5 %collective-permute-start.2 = (f32[128,100]{0,1:T(8,128)S(1)}, f32[128,100]{0,1:T(8,128)S(1)}, u32[]{:S(2)}, u32[]{:S(2)}) collective-permute-start(f32[128,100]{0,1:T(8,128)S(1)} %pad_maximum_fusion), channel_id=1, source_target_pairs={{0,4},{2,6},{4,0},{6,2},{8,12},{10,14},{12,8},{14,10},{16,20},{18,... | collective-permute-start | bytes 153608 | tf_op jit(solution)/shard_map/ppermute | solution.py:12
  23.0 0.6 %collective-permute-done.1 = f32[128,100]{0,1:T(8,128)S(1)} collective-permute-done((f32[128,100]{0,1:T(8,128)S(1)}, f32[128,100]{0,1:T(8,128)S(1)}, u32[]{:S(2)}, u32[]{:S(2)}) %collective-permute-start.1) | collective-permute-done | bytes 51232 | tf_op jit(solution)/shard_map/ppermute | solution.py:12
  23.6 2.0 %collective-permute-done.2 = f32[128,100]{0,1:T(8,128)S(1)} collective-permute-done((f32[128,100]{0,1:T(8,128)S(1)}, f32[128,100]{0,1:T(8,128)S(1)}, u32[]{:S(2)}, u32[]{:S(2)}) %collective-permute-start.2) | collective-permute-done | bytes 51232 | tf_op jit(solution)/shard_map/ppermute | solution.py:12
  25.6 2.4 %collective-permute-done.3 = f32[128,100]{0,1:T(8,128)S(1)} collective-permute-done((f32[128,100]{0,1:T(8,128)S(1)}, f32[128,100]{0,1:T(8,128)S(1)}, u32[]{:S(2)}, u32[]{:S(2)}) %collective-permute-start.3) | collective-permute-done | bytes 51232 | tf_op jit(solution)/shard_map/ppermute | solution.py:12
  28.0 1.6 %collective-permute-start.4 = (f32[128,100]{0,1:T(8,128)S(1)}, f32[128,100]{0,1:T(8,128)S(1)}, u32[]{:S(2)}, u32[]{:S(2)}) collective-permute-start(f32[128,100]{0,1:T(8,128)S(1)} %add_add_fusion.1), channel_id=1, source_target_pairs={{0,8},{2,10},{4,12},{6,14},{8,0},{10,2},{12,4},{14,6},{16,24},{18,... | collective-permute-start | bytes 153608 | tf_op jit(solution)/shard_map/ppermute | solution.py:12
  29.6 2.6 %collective-permute-start.5 = (f32[128,100]{0,1:T(8,128)S(1)}, f32[128,100]{0,1:T(8,128)S(1)}, u32[]{:S(2)}, u32[]{:S(2)}) collective-permute-start(f32[128,100]{0,1:T(8,128)S(1)} %add_add_fusion.1), channel_id=1, source_target_pairs={{0,16},{2,18},{4,20},{6,22},{8,24},{10,26},{12,28},{14,30},{16,0},... | collective-permute-start | bytes 153608 | tf_op jit(solution)/shard_map/ppermute | solution.py:12
  32.2 0.2 collective-permute-start.6
  32.5 2.3 %multiply_reduce_fusion = bf16[128,512]{1,0:T(8,128)(2,1)S(1)} fusion(bf16[128,60,512]{2,0,1:T(8,128)(2,1)S(1)} %copy-done, f32[60,512]{1,0:T(8,128)S(1)} %fusion.12), kind=kLoop, calls=%fused_computation | loop fusion | flops 11730944 | bytes 8118272 | tf_op jit(solution)/shard_map/reduce_sum | solution.py:43
  34.8 1.0 %collective-permute-done.5 = f32[128,100]{0,1:T(8,128)S(1)} collective-permute-done((f32[128,100]{0,1:T(8,128)S(1)}, f32[128,100]{0,1:T(8,128)S(1)}, u32[]{:S(2)}, u32[]{:S(2)}) %collective-permute-start.5) | collective-permute-done | bytes 51232 | tf_op jit(solution)/shard_map/ppermute | solution.py:12
  35.8 2.3 %collective-permute-done.6 = f32[128,100]{0,1:T(8,128)S(1)} collective-permute-done((f32[128,100]{0,1:T(8,128)S(1)}, f32[128,100]{0,1:T(8,128)S(1)}, u32[]{:S(2)}, u32[]{:S(2)}) %collective-permute-start.6) | collective-permute-done | bytes 51232 | tf_op jit(solution)/shard_map/ppermute | solution.py:12
  38.2 0.1 collective-permute-start.7
  38.3 0.6 %maximum_select_fusion = f32[128,100]{0,1:T(8,128)} fusion(f32[128,100]{0,1:T(8,128)S(1)} %add_add_fusion, f32[128,50]{0,1:T(8,128)S(1)} %get-tuple-element.5, f32[128,50]{0,1:T(8,128)S(1)} %get-tuple-element.4, pred[]{:T(512)S(6)} %eq.3), kind=kLoop, calls=%fused_computation.16 | loop fusion | flops 25600 | bytes 153601 | tf_op jit(solution)/shard_map/jit(_where)/select_n | solution.py:55
  38.9 0.5 %collective-permute-done.7 = bf16[128,50]{0,1:T(8,128)(2,1)S(1)} collective-permute-done((bf16[128,50]{0,1:T(8,128)(2,1)S(1)}, bf16[128,50]{0,1:T(8,128)(2,1)S(1)}, u32[]{:S(2)}, u32[]{:S(2)}) %collective-permute-start.7) | collective-permute-done | bytes 12832 | tf_op jit(solution)/shard_map/ppermute | solution.py:29
  39.5 0.1 fusion.17
  39.6 0.8 %fusion.4 = f32[50,512]{1,0:T(8,128)} fusion(f32[50,512]{1,0:T(8,128)S(1)} %fusion.17, bf16[128,512]{1,0:T(8,128)(2,1)S(1)} %multiply_reduce_fusion, f32[128,100]{0,1:T(8,128)S(1)} %add_add_fusion), kind=kOutput, calls=%fused_computation.8 | convolution fusion | flops 6604800 | bytes 362496 | tf_op jit(solution)/shard_map/dot_general | solution.py:57
  (14 shorter events, 0.2 us)
Async XLA Ops:
  0.6 6.2 %collective-permute-start = (bf16[50,60,512]{2,1,0:T(8,128)(2,1)}, bf16[50,60,512]{2,1,0:T(8,128)(2,1)S(1)}, u32[]{:S(2)}, u32[]{:S(2)}) collective-permute-start(bf16[50,60,512]{2,1,0:T(8,128)(2,1)} %param.6), channel_id=1, source_target_pairs={{0,1},{1,0},{2,3},{3,2},{4,5},{5,4},{6,7},{7,6},{8,9},{9,8},{10,11... | collective-permute-start | bytes 9216008 | tf_op jit(solution)/shard_map/ppermute | solution.py:29
  3.8 6.7 %copy-start = (bf16[128,60,512]{2,0,1:T(8,128)(2,1)S(1)}, bf16[128,60,512]{2,0,1:T(8,128)(2,1)}, u32[]{:S(2)}) copy-start(bf16[128,60,512]{2,0,1:T(8,128)(2,1)} %param.5) | copy-start | bytes 23592964
  14.5 8.5 %copy-start.1 = (s32[512]{0:T(512)S(1)}, s32[512]{0:T(512)}, u32[]{:S(2)}) copy-start(s32[512]{0:T(512)} %param.8) | copy-start | bytes 6148
  18.5 5.0 %collective-permute-start.1 = (f32[128,100]{0,1:T(8,128)S(1)}, f32[128,100]{0,1:T(8,128)S(1)}, u32[]{:S(2)}, u32[]{:S(2)}) collective-permute-start(f32[128,100]{0,1:T(8,128)S(1)} %pad_maximum_fusion), channel_id=1, source_target_pairs={{0,2},{2,0},{4,6},{6,4},{8,10},{10,8},{12,14},{14,12},{16,18},{18,... | collective-permute-start | bytes 153608 | tf_op jit(solution)/shard_map/ppermute | solution.py:12
  21.4 4.1 %collective-permute-start.2 = (f32[128,100]{0,1:T(8,128)S(1)}, f32[128,100]{0,1:T(8,128)S(1)}, u32[]{:S(2)}, u32[]{:S(2)}) collective-permute-start(f32[128,100]{0,1:T(8,128)S(1)} %pad_maximum_fusion), channel_id=1, source_target_pairs={{0,4},{2,6},{4,0},{6,2},{8,12},{10,14},{12,8},{14,10},{16,20},{18,... | collective-permute-start | bytes 153608 | tf_op jit(solution)/shard_map/ppermute | solution.py:12
  22.9 5.0 %collective-permute-start.3 = (f32[128,100]{0,1:T(8,128)S(1)}, f32[128,100]{0,1:T(8,128)S(1)}, u32[]{:S(2)}, u32[]{:S(2)}) collective-permute-start(f32[128,100]{0,1:T(8,128)S(1)} %pad_maximum_fusion), channel_id=1, source_target_pairs={{0,6},{2,4},{4,2},{6,0},{8,14},{10,12},{12,10},{14,8},{16,22},{18,... | collective-permute-start | bytes 153608 | tf_op jit(solution)/shard_map/ppermute | solution.py:12
  28.0 6.8 %collective-permute-start.4 = (f32[128,100]{0,1:T(8,128)S(1)}, f32[128,100]{0,1:T(8,128)S(1)}, u32[]{:S(2)}, u32[]{:S(2)}) collective-permute-start(f32[128,100]{0,1:T(8,128)S(1)} %add_add_fusion.1), channel_id=1, source_target_pairs={{0,8},{2,10},{4,12},{6,14},{8,0},{10,2},{12,4},{14,6},{16,24},{18,... | collective-permute-start | bytes 153608 | tf_op jit(solution)/shard_map/ppermute | solution.py:12
  29.6 6.2 %collective-permute-start.5 = (f32[128,100]{0,1:T(8,128)S(1)}, f32[128,100]{0,1:T(8,128)S(1)}, u32[]{:S(2)}, u32[]{:S(2)}) collective-permute-start(f32[128,100]{0,1:T(8,128)S(1)} %add_add_fusion.1), channel_id=1, source_target_pairs={{0,16},{2,18},{4,20},{6,22},{8,24},{10,26},{12,28},{14,30},{16,0},... | collective-permute-start | bytes 153608 | tf_op jit(solution)/shard_map/ppermute | solution.py:12
  32.2 5.9 %collective-permute-start.6 = (f32[128,100]{0,1:T(8,128)S(1)}, f32[128,100]{0,1:T(8,128)S(1)}, u32[]{:S(2)}, u32[]{:S(2)}) collective-permute-start(f32[128,100]{0,1:T(8,128)S(1)} %add_add_fusion.1), channel_id=1, source_target_pairs={{0,24},{2,26},{4,28},{6,30},{8,16},{10,18},{12,20},{14,22},{16,8},... | collective-permute-start | bytes 153608 | tf_op jit(solution)/shard_map/ppermute | solution.py:12
  34.7 4.2 %collective-permute-start.8 = (bf16[128,512]{1,0:T(8,128)(2,1)S(1)}, bf16[128,512]{1,0:T(8,128)(2,1)S(1)}, u32[]{:S(2)}, u32[]{:S(2)}) collective-permute-start(bf16[128,512]{1,0:T(8,128)(2,1)S(1)} %multiply_reduce_fusion), channel_id=1, source_target_pairs={{0,1},{1,0},{2,3},{3,2},{4,5},{5,4},{6,7},{7,6},{8,9},{9,8},{10,11... | collective-permute-start | bytes 393224 | tf_op jit(solution)/shard_map/ppermute | solution.py:29
  38.2 1.2 %collective-permute-start.7 = (bf16[128,50]{0,1:T(8,128)(2,1)S(1)}, bf16[128,50]{0,1:T(8,128)(2,1)S(1)}, u32[]{:S(2)}, u32[]{:S(2)}) collective-permute-start(bf16[128,50]{0,1:T(8,128)(2,1)S(1)} %slice.15), channel_id=1, source_target_pairs={{0,1},{1,0},{2,3},{3,2},{4,5},{5,4},{6,7},{7,6},{8,9},{9,8},{10,11... | collective-permute-start | bytes 38408 | tf_op jit(solution)/shard_map/ppermute | solution.py:29
